TPU v7x, 256 devices: a whole 4x4x8 slice. The times are simulated.
256 devices in a mesh: expert: 64 (over z, y, core), tensor: 4 (over x).
Axes of the slice: x: 4, y: 4, z: 8, core: 2. Of those that a mesh axis runs over, the one named last changes fastest.
Arguments:
- context: bfloat16 [8192, 4096], P('expert', 'tensor'), may hold values from -6 to 6
- residual_in: bfloat16 [8192, 4096], P('expert')
- out_weight: bfloat16 [4096, 4096], P('tensor', 'expert'), may hold values from -0.09375 to 0.09375
- norm_gain: bfloat16 [4096], replicated, may hold values from 0.099609375 to 1.8984375
- expert_ids: int32 [8192, 8], P('expert'), may hold values from 0 to 63, all different within a row; in each aligned block of 128 rows (0 to 127, 128 to 255, ...) at most 18 rows name the same one
- gate_weights: float32 [8192, 8], P('expert'), may hold values from 0.1 to 1
- gate_matrix: bfloat16 [64, 4096, 1536], P('expert', None, 'tensor'), may hold values from -0.09375 to 0.09375
- lift_matrix: bfloat16 [64, 4096, 1536], P('expert', None, 'tensor'), may hold values from -0.09375 to 0.09375
- down_matrix: bfloat16 [64, 1536, 4096], P('expert', 'tensor'), may hold values from -0.15625 to 0.15625
Outputs:
- layer_out: bfloat16 [8192, 4096], P('expert', 'tensor')
Inputs may be any that keep to these rules, and one draw needn't show every extreme that they name: `expert_ids`: each row names 8 different experts. Within each aligned block of 128 rows (the rows of one index of the expert axis) no expert is named more than 18 times, a bound that some block reaches.
All inputs are finite; a program needn't handle non-finite values.
Results may differ from a plain program's by a relative error of at most 0.009.
Values may be sent and summed in bfloat16 or wider, within the bound.
No kernel may reach another device: no remote copies, remote signals or barrier semaphores. Data moves between devices by JAX's collectives and lax.ppermute only.
A program may use at most 128 MiB of HBM per device.

v0:
```python
import jax
import jax.numpy as jnp
from jax import lax
from jax.sharding import PartitionSpec as P

epsilon = 1e-06


def body(
    context,
    residual_in,
    out_weight,
    norm_gain,
    expert_ids,
    gate_weights,
    gate_matrix,
    lift_matrix,
    down_matrix,
):
    tokens_here, model_width = residual_in.shape
    top_count = expert_ids.shape[1]
    share_width = model_width // lax.axis_size("tensor")
    column_start = lax.axis_index("tensor") * share_width
    experts_all = lax.axis_size("expert") * gate_matrix.shape[0]
    capacity = min(tokens_here, max(2, tokens_here * top_count * 9 // (8 * experts_all)))
    attention_part = jnp.dot(
        context,
        lax.all_gather(out_weight, "expert", axis=1, tiled=True),
        preferred_element_type=jnp.float32,
    )
    attention_out = lax.psum(attention_part, "tensor")
    hidden_state = (residual_in.astype(jnp.float32) + attention_out).astype(jnp.bfloat16)
    widened = hidden_state.astype(jnp.float32)
    squares_mean = jnp.mean(widened * widened, axis=1, keepdims=True)
    normed_full = (
        widened * lax.rsqrt(squares_mean + epsilon) * norm_gain.astype(jnp.float32)
    ).astype(jnp.bfloat16)
    hidden_share = lax.dynamic_slice_in_dim(hidden_state, column_start, share_width, 1)
    flat_ids = expert_ids.reshape(-1)
    onehot_table = (flat_ids[:, None] == jnp.arange(experts_all, dtype=jnp.int32)[None, :]).astype(
        jnp.int32
    )
    earlier = jnp.cumsum(onehot_table, axis=0) - onehot_table
    slot_index = jnp.sum(earlier * onehot_table, axis=1)
    destination = flat_ids * capacity + slot_index
    token_index = jnp.arange(tokens_here * top_count, dtype=jnp.int32) // top_count
    source_width = normed_full.shape[1]
    buffer_rows = jnp.zeros((experts_all * capacity, source_width), jnp.bfloat16)
    buffer_rows = buffer_rows.at[destination].set(normed_full[token_index])
    buffer_rows = buffer_rows.reshape(experts_all, capacity, source_width)
    received = lax.all_to_all(buffer_rows, "expert", split_axis=0, concat_axis=0, tiled=True)
    senders = received.shape[0]
    slots_here = received.shape[1]
    flat_rows = received.reshape(senders * slots_here, model_width)
    gate_values = jnp.dot(flat_rows, gate_matrix[0], preferred_element_type=jnp.float32)
    lift_values = jnp.dot(flat_rows, lift_matrix[0], preferred_element_type=jnp.float32)
    activation = (jax.nn.silu(gate_values) * lift_values).astype(jnp.bfloat16)
    partial_out = jnp.dot(activation, down_matrix[0], preferred_element_type=jnp.float32)
    expert_partial = partial_out.reshape(senders, slots_here, model_width)
    expert_share = lax.psum_scatter(
        expert_partial.astype(jnp.bfloat16), "tensor", scatter_dimension=2, tiled=True
    )
    returned = lax.all_to_all(expert_share, "expert", split_axis=0, concat_axis=0, tiled=True)
    picked = returned.reshape(experts_all * capacity, share_width)[destination]
    picked = picked.reshape(tokens_here, top_count, share_width)
    moe_share = jnp.sum(gate_weights[:, :, None] * picked.astype(jnp.float32), axis=1)
    return (hidden_share.astype(jnp.float32) + moe_share).astype(jnp.bfloat16)


def solution(mesh):
    placed = (
        P("expert", "tensor"),
        P("expert", None),
        P("tensor", "expert"),
        P(),
        P("expert", None),
        P("expert", None),
        P("expert", None, "tensor"),
        P("expert", None, "tensor"),
        P("expert", "tensor", None),
    )
    return jax.shard_map(
        body, mesh=mesh, in_specs=placed, out_specs=P("expert", "tensor"), check_vma=False
    )
```

profile of v0, /device:TPU:8, one launch (start us, length us, event | category | flops | bytes accessed | tf_op | source)
XLA Modules:
  0.0 744.2 jit_solution(13246930377981361659)
XLA Ops:
  6.5 0.0 copy-start
  6.5 0.0 all-gather.2.cloned.1.call-start
  6.5 0.7 all-gather.2.cloned.1.call-update
  7.3 0.0 copy-start.3
  7.3 0.0 all-reduce.2.cloned.1.call-start
  7.3 87.5 %all-gather.2.cloned.1.call-done = bf16[1024,4096]{0,1:T(8,128)(2,1)} async-done(((bf16[1024,64]{0,1:T(8,128)(2,1)}), bf16[1024,4096]{0,1:T(8,128)(2,1)}) %all-gather.2.cloned.1.call-update) | async-done | bytes 8388624 | tf_op jit(solution)/shard_map/all_gather | solution.py:28
  94.8 7.7 %fusion.18 = f32[128,4096]{1,0:T(8,128)} fusion(bf16[128,1024]{1,0:T(8,128)(2,1)} %param.9, bf16[1024,4096]{0,1:T(8,128)(2,1)} %all-gather.2.cloned.1.call-done), kind=kOutput, calls=%fused_computation.40 | convolution fusion | flops 1073741824 | bytes 10747904 | tf_op jit(solution)/shard_map/dot_general | solution.py:26
  102.5 0.0 copy-start.4
  102.5 0.0 all-reduce.2.cloned.1.call-update
  102.6 0.0 reduce-scatter.2.cloned.1.call-start
  102.6 0.0 copy-done.3
  102.6 0.1 copy.22
  102.7 0.1 eq.29
  102.8 0.1 eq.25
  102.9 0.7 fusion.17
  103.6 31.1 %reduce-window.6 = s32[64,8,128]{2,1,0:T(8,128)S(1)} reduce-window(s32[64,8,128]{2,1,0:T(8,128)} %fusion.17, s32[]{:T(128)} %constant.17.clone.1), window={size=1x1x128 pad=0_0x0_0x127_0}, to_apply=%region_1.0 | reduce-window | flops 8323072 | bytes 524292 | tf_op jit(solution)/shard_map/reduce-window
  134.7 0.8 slice.12
  135.6 1.1 copy.24
  136.7 0.1 copy.25
  136.8 0.1 copy.21
  136.9 0.1 mul.60
  137.0 0.0 copy-done.4
  137.0 0.1 broadcast_add_fusion
  137.2 0.1 fusion.16
  137.3 27.9 %all-reduce.2.cloned.1.call-done = f32[128,4096]{1,0:T(8,128)} async-done(((f32[128,4096]{1,0:T(8,128)}), f32[128,4096]{1,0:T(8,128)}) %all-reduce.2.cloned.1.call-update) | async-done | bytes 2097168 | tf_op jit(solution)/shard_map/psum | solution.py:31
  165.1 2.3 fusion.10
  167.4 0.0 copy-start.2
  167.4 1.1 copy-done.2
  168.5 1.4 fusion.12
  169.9 16.4 %gather_fusion = bf16[1024,4096]{1,0:T(8,128)(2,1)} fusion(bf16[128,4096]{1,0:T(8,128)(2,1)} %fusion.12, s32[1024]{0:T(1024)S(1)} %broadcast_clamp_fusion.1), kind=kCustom, calls=%fused_computation | custom fusion | bytes 16781312 | tf_op jit(solution)/shard_map/gather | solution.py:49
  186.3 18.2 %scatter_custom_fusion = bf16[1152,4096]{1,0:T(8,128)(2,1)} fusion(s32[1024]{0:T(1024)S(1)} %bitcast.43, bf16[1024,4096]{1,0:T(8,128)(2,1)} %gather_fusion, bf16[]{:T(256)} %constant.38.clone.1), kind=kCustom, calls=%fused_computation.4 | custom fusion | bytes 9437696 | tf_op jit(solution)/shard_map/scatter | solution.py:49
  204.5 13.9 %reshape.114 = bf16[64,18,4096]{2,1,0:T(8,128)(2,1)} reshape(bf16[1152,4096]{1,0:T(8,128)(2,1)} %scatter_custom_fusion) | data formatting | bytes 18874368 | tf_op jit(solution)/shard_map/reshape | solution.py:50
  218.4 286.6 %all_to_all.10 = bf16[64,18,4096]{2,1,0:T(8,128)(2,1)} all-to-all(bf16[64,18,4096]{2,1,0:T(8,128)(2,1)} %reshape.114), channel_id=1, replica_groups=mesh['expert'=64,'tensor'=4] {'expert'}, dimensions={0} | all-to-all | bytes 18874368 | tf_op jit(solution)/shard_map/all_to_all | solution.py:51
  505.0 14.2 %reshape.115 = bf16[1152,4096]{1,0:T(8,128)(2,1)} reshape(bf16[64,18,4096]{2,1,0:T(8,128)(2,1)} %all_to_all.10) | data formatting | bytes 18874368 | tf_op jit(solution)/shard_map/reshape | solution.py:54
  519.2 0.0 copy-start.1
  519.2 0.0 copy-start.6
  519.2 8.7 %fusion.5 = f32[1152,384]{1,0:T(8,128)S(1)} fusion(bf16[1152,4096]{1,0:T(8,128)(2,1)} %reshape.115, bf16[1,4096,384]{2,1,0:T(8,128)(2,1)} %param.15), kind=kOutput, calls=%fused_computation.11 | convolution fusion | flops 3623878656 | bytes 14352384 | tf_op jit(solution)/shard_map/dot_general | solution.py:55
  527.9 0.0 copy-done.1
  527.9 0.0 copy-done.6
  527.9 6.2 fusion.7
  534.1 2.2 dot_general.17
  536.3 0.0 copy-done
  536.3 8.7 %convolution_convert_fusion = bf16[64,18,4096]{2,0,1:T(8,128)(2,1)} fusion(bf16[1,384,4096]{2,1,0:T(8,128)(2,1)S(1)} %copy-done, bf16[64,18,384]{2,1,0:T(8,128)(2,1)} %dot_general.17), kind=kOutput, calls=%fused_computation.3 | convolution fusion | flops 3628597248 | bytes 13467648 | tf_op jit(solution)/shard_map/dot_general | solution.py:58
  545.0 0.0 reduce-scatter.2.cloned.1.call-update
  545.0 86.4 %reduce-scatter.2.cloned.1.call-done = bf16[64,18,1024]{2,0,1:T(8,128)(2,1)} async-done(((bf16[64,18,4096]{2,0,1:T(8,128)(2,1)}), bf16[64,18,1024]{2,0,1:T(8,128)(2,1)}) %reduce-scatter.2.cloned.1.call-update) | async-done | bytes 2359312 | tf_op jit(solution)/shard_map/reduce_scatter | solution.py:60
  631.4 4.7 copy.27
  636.2 0.0 copy-start.5
  636.2 10.9 %all-to-all-start.1 = ((bf16[64,18,1024]{2,1,0:T(8,128)(2,1)}), bf16[64,18,1024]{2,1,0:T(8,128)(2,1)}, u32[]{:S(2)}, u32[]{:S(2)}) async-start(bf16[64,18,1024]{2,1,0:T(8,128)(2,1)} %copy.27), calls=%async_computation.2 | async-start | bytes 6291456 | tf_op jit(solution)/shard_map/all_to_all | solution.py:63
  647.0 0.0 copy-done.5
  647.0 0.1 copy.20
  647.2 73.5 %all-to-all-done.1 = bf16[64,18,1024]{2,1,0:T(8,128)(2,1)} async-done(((bf16[64,18,1024]{2,1,0:T(8,128)(2,1)}), bf16[64,18,1024]{2,1,0:T(8,128)(2,1)}, u32[]{:S(2)}, u32[]{:S(2)}) %all-to-all-start.1) | async-done | bytes 2359328 | tf_op jit(solution)/shard_map/all_to_all | solution.py:63
  720.7 4.3 reshape.116
  725.0 8.0 %gather_fusion.1 = bf16[1024,1024]{1,0:T(8,128)(2,1)} fusion(bf16[1152,1024]{1,0:T(8,128)(2,1)} %reshape.116, s32[1024]{0:T(1024)S(1)} %broadcast_clamp_fusion), kind=kCustom, calls=%fused_computation.1 | custom fusion | bytes 4198400 | tf_op jit(solution)/shard_map/gather | solution.py:64
  733.0 2.9 fusion.2
  735.9 1.7 add_convert_fusion.1
  (9 shorter events, 0.1 us)
Async XLA Ops:
  6.5 529.8 %copy-start = (bf16[1,384,4096]{2,1,0:T(8,128)(2,1)S(1)}, bf16[1,384,4096]{2,1,0:T(8,128)(2,1)}, u32[]{:S(2)}) copy-start(bf16[1,384,4096]{2,1,0:T(8,128)(2,1)} %param.17) | copy-start | bytes 9437188
  6.5 88.3 %all-gather.2.cloned.1.call-start = ((), (), s32[]{:S(2)}) async-start(), calls=%async_computation.3 | async-start | bytes 8519680 | tf_op jit(solution)/shard_map/all_gather | solution.py:28
  7.3 95.3 %copy-start.3 = (s32[128,8]{0,1:T(8,128)S(1)}, s32[128,8]{0,1:T(8,128)}, u32[]{:S(2)}) copy-start(s32[128,8]{0,1:T(8,128)} %param.13) | copy-start | bytes 12292
  7.3 157.9 %all-reduce.2.cloned.1.call-start = ((), (), s32[]{:S(2)}) async-start(), calls=%async_computation.4 | async-start | bytes 4194304 | tf_op jit(solution)/shard_map/psum | solution.py:31
  102.5 34.5 %copy-start.4 = (bf16[4096]{0:T(1024)(128)(2,1)S(1)}, bf16[4096]{0:T(1024)(128)(2,1)}, u32[]{:S(2)}) copy-start(bf16[4096]{0:T(1024)(128)(2,1)} %param.12) | copy-start | bytes 24580
  102.6 528.9 %reduce-scatter.2.cloned.1.call-start = ((), (), s32[]{:S(2)}) async-start(), calls=%async_computation.5 | async-start | bytes 11796480 | tf_op jit(solution)/shard_map/reduce_scatter | solution.py:60
  167.4 1.1 copy-start.2
  519.2 8.7 %copy-start.1 = (bf16[1152,4096]{1,0:T(8,128)(2,1)S(1)}, bf16[1152,4096]{1,0:T(8,128)(2,1)}, u32[]{:S(2)}) copy-start(bf16[1152,4096]{1,0:T(8,128)(2,1)} %reshape.115) | copy-start | bytes 28311556
  519.2 8.7 %copy-start.6 = (bf16[1,4096,384]{2,1,0:T(8,128)(2,1)S(1)}, bf16[1,4096,384]{2,1,0:T(8,128)(2,1)}, u32[]{:S(2)}) copy-start(bf16[1,4096,384]{2,1,0:T(8,128)(2,1)} %param.16) | copy-start | bytes 9437188
  636.2 10.9 %copy-start.5 = (f32[128,8]{0,1:T(8,128)S(1)}, f32[128,8]{0,1:T(8,128)}, u32[]{:S(2)}) copy-start(f32[128,8]{0,1:T(8,128)} %param.14) | copy-start | bytes 12292
  636.2 84.5 %all-to-all-start.1 = ((bf16[64,18,1024]{2,1,0:T(8,128)(2,1)}), bf16[64,18,1024]{2,1,0:T(8,128)(2,1)}, u32[]{:S(2)}, u32[]{:S(2)}) async-start(bf16[64,18,1024]{2,1,0:T(8,128)(2,1)} %copy.27), calls=%async_computation.2 | async-start | bytes 6291456 | tf_op jit(solution)/shard_map/all_to_all | solution.py:63
Sparse Core Ops, SparseCore 0:
  10.1 84.6 all-gather.1
  102.7 62.4 all-reduce.1
  545.1 86.2 reduce-scatter.1
where the time goes:
time: 747 us; the launch traced here: 744 us
  blocking collectives  287 us (38%)
  waiting for transfers between devices  276 us (37%)
  local copies, waits for them, and re-layouts  85.7 us (11%)
  other arithmetic  40.4 us (5%)
  matrix products  31.3 us (4%)
  between operations  13.3 us (2%)
  starting transfers between devices  11 us (1%)
    all_to_all x1, blocking collectives, body(): lax.all_to_all(buffer_rows, 'expert', split_axis=0, concat_axis=0, tiled=...  287 us
    all_gather x1, waiting for transfers between devices, body(): lax.all_gather(out_weight, 'expert', axis=1, tiled=True)  87.5 us
    reduce_scatter x1, waiting for transfers between devices, body(): lax.psum_scatter(expert_partial.astype(jnp.bfloat16), 'tensor', scatter_d...  86.4 us
    all_to_all x1, waiting for transfers between devices, body(): lax.all_to_all(expert_share, 'expert', split_axis=0, concat_axis=0, tiled...  73.5 us
    another operation x3, other arithmetic  31.3 us
    psum x1, waiting for transfers between devices, body(): attention_out = lax.psum(attention_part, 'tensor')  27.9 us
    scatter x1, local copies, waits for them, and re-layouts, body(): buffer_rows = buffer_rows.at[destination].set(normed_full[token_index])  18.2 us
    gather x1, local copies, waits for them, and re-layouts, body(): buffer_rows = buffer_rows.at[destination].set(normed_full[token_index])  16.4 us
  transfers between devices with their start and end apart: 4, of which 4 were waited for; matrix products, arithmetic and copies ran while one was open for 5% of the time, Pallas kernels for 0%

commit v1 on v0

--- a/solution.py
+++ b/solution.py
@@ -28,7 +28,11 @@
         lax.all_gather(out_weight, "expert", axis=1, tiled=True),
         preferred_element_type=jnp.float32,
     )
-    attention_out = lax.psum(attention_part, "tensor")
+    attention_out = attention_part
+    for hop in (1, 2):
+        attention_out = attention_out + lax.ppermute(
+            attention_out, "tensor", [(dev, dev ^ hop) for dev in range(4)]
+        )
     hidden_state = (residual_in.astype(jnp.float32) + attention_out).astype(jnp.bfloat16)
     widened = hidden_state.astype(jnp.float32)
     squares_mean = jnp.mean(widened * widened, axis=1, keepdims=True)

time: 747 us -> 781 us (1.046)
  waiting for transfers between devices: 276 us -> 307 us
    ppermute x0 -> x2, waiting for transfers between devices: none -> 57.5 us  [body(): lax.ppermute(attention_out, 'tensor', [(dev, dev ^ hop) for dev in range(...]
    psum x1 -> x0, waiting for transfers between devices: 27.9 us -> none  [body(): attention_out = lax.psum(attention_part, 'tensor')]
  transfers between devices with their start and end apart: 4 -> 5, of which waited for: 4 -> 5; matrix products, arithmetic and copies ran while one was open for 5% -> 4% of each run, Pallas kernels for 0% -> 0%
where the time goes in v1:
time: 781 us; the launch traced here: 778 us
  waiting for transfers between devices  307 us (39%)
  blocking collectives  284 us (36%)
  local copies, waits for them, and re-layouts  85.7 us (11%)
  other arithmetic  42.8 us (5%)
  matrix products  29.9 us (4%)
  starting transfers between devices  15.4 us (2%)
  between operations  13.6 us (2%)
    all_to_all x1, blocking collectives, body(): lax.all_to_all(buffer_rows, 'expert', split_axis=0, concat_axis=0, tiled=...  284 us
    reduce_scatter x1, waiting for transfers between devices, body(): lax.psum_scatter(expert_partial.astype(jnp.bfloat16), 'tensor', scatter_d...  87.9 us
    all_gather x1, waiting for transfers between devices, body(): lax.all_gather(out_weight, 'expert', axis=1, tiled=True)  87.5 us
    all_to_all x1, waiting for transfers between devices, body(): lax.all_to_all(expert_share, 'expert', split_axis=0, concat_axis=0, tiled...  73.5 us
    ppermute x2, waiting for transfers between devices, body(): lax.ppermute(attention_out, 'tensor', [(dev, dev ^ hop) for dev in range(...  57.5 us
    another operation x3, other arithmetic  31.3 us
    scatter x1, local copies, waits for them, and re-layouts, body(): buffer_rows = buffer_rows.at[destination].set(normed_full[token_index])  18.2 us
    gather x1, local copies, waits for them, and re-layouts, body(): buffer_rows = buffer_rows.at[destination].set(normed_full[token_index])  16.4 us
  transfers between devices with their start and end apart: 5, of which 5 were waited for; matrix products, arithmetic and copies ran while one was open for 4% of the time, Pallas kernels for 0%

profile of v1, /device:TPU:8, one launch (start us, length us, event | category | flops | bytes accessed | tf_op | source)
XLA Modules:
  0.0 778.4 jit_solution(16607378935649140922)
XLA Ops:
  6.5 0.0 copy-start
  6.5 0.0 all-gather.2.cloned.1.call-start
  6.5 0.7 all-gather.2.cloned.1.call-update
  7.3 0.0 reduce-scatter.2.cloned.1.call-start
  7.3 87.5 %all-gather.2.cloned.1.call-done = bf16[1024,4096]{0,1:T(8,128)(2,1)} async-done(((bf16[1024,64]{0,1:T(8,128)(2,1)}), bf16[1024,4096]{0,1:T(8,128)(2,1)}) %all-gather.2.cloned.1.call-update) | async-done | bytes 8388624 | tf_op jit(solution)/shard_map/all_gather | solution.py:28
  94.8 6.3 fusion.18
  101.1 0.0 copy-start.3
  101.2 0.0 copy-start.4
  101.2 1.6 collective-permute-start
  102.7 46.3 %collective-permute-done = f32[128,4096]{1,0:T(8,128)S(1)} collective-permute-done((f32[128,4096]{1,0:T(8,128)S(1)}, f32[128,4096]{1,0:T(8,128)S(1)}, u32[]{:S(2)}, u32[]{:S(2)}) %collective-permute-start) | collective-permute-done | bytes 2097184 | tf_op jit(solution)/shard_map/ppermute | solution.py:33
  149.1 1.7 add.74
  150.7 3.0 collective-permute-start.1
  153.7 0.0 copy-done.3
  153.7 0.1 copy.22
  153.8 0.1 eq.29
  153.9 0.1 eq.25
  154.0 0.0 copy-done.4
  154.0 0.7 fusion.17
  154.7 31.1 %reduce-window.6 = s32[64,8,128]{2,1,0:T(8,128)S(1)} reduce-window(s32[64,8,128]{2,1,0:T(8,128)} %fusion.17, s32[]{:T(128)} %constant.17.clone.1), window={size=1x1x128 pad=0_0x0_0x127_0}, to_apply=%region_0.0 | reduce-window | flops 8323072 | bytes 524292 | tf_op jit(solution)/shard_map/reduce-window
  185.8 0.8 slice.12
  186.7 1.1 copy.24
  187.8 0.1 copy.25
  187.9 0.1 copy.21
  188.0 0.1 mul.60
  188.1 0.1 broadcast_add_fusion
  188.2 0.1 fusion.16
  188.3 11.2 %collective-permute-done.1 = f32[128,4096]{1,0:T(8,128)} collective-permute-done((f32[128,4096]{1,0:T(8,128)}, f32[128,4096]{1,0:T(8,128)}, u32[]{:S(2)}, u32[]{:S(2)}) %collective-permute-start.1) | collective-permute-done | bytes 2097184 | tf_op jit(solution)/shard_map/ppermute | solution.py:33
  199.5 3.0 fusion.10
  202.5 0.0 copy-start.2
  202.6 1.1 copy-done.2
  203.6 1.4 fusion.12
  205.0 16.4 %gather_fusion = bf16[1024,4096]{1,0:T(8,128)(2,1)} fusion(bf16[128,4096]{1,0:T(8,128)(2,1)} %fusion.12, s32[1024]{0:T(1024)S(1)} %broadcast_clamp_fusion.1), kind=kCustom, calls=%fused_computation | custom fusion | bytes 16781312 | tf_op jit(solution)/shard_map/gather | solution.py:53
  221.4 18.2 %scatter_custom_fusion = bf16[1152,4096]{1,0:T(8,128)(2,1)} fusion(s32[1024]{0:T(1024)S(1)} %bitcast.43, bf16[1024,4096]{1,0:T(8,128)(2,1)} %gather_fusion, bf16[]{:T(256)} %constant.38.clone.1), kind=kCustom, calls=%fused_computation.4 | custom fusion | bytes 9437696 | tf_op jit(solution)/shard_map/scatter | solution.py:53
  239.6 13.9 %reshape.114 = bf16[64,18,4096]{2,1,0:T(8,128)(2,1)} reshape(bf16[1152,4096]{1,0:T(8,128)(2,1)} %scatter_custom_fusion) | data formatting | bytes 18874368 | tf_op jit(solution)/shard_map/reshape | solution.py:54
  253.5 283.9 %all_to_all.10 = bf16[64,18,4096]{2,1,0:T(8,128)(2,1)} all-to-all(bf16[64,18,4096]{2,1,0:T(8,128)(2,1)} %reshape.114), channel_id=1, replica_groups=mesh['expert'=64,'tensor'=4] {'expert'}, dimensions={0} | all-to-all | bytes 18874368 | tf_op jit(solution)/shard_map/all_to_all | solution.py:55
  537.4 14.2 %reshape.115 = bf16[1152,4096]{1,0:T(8,128)(2,1)} reshape(bf16[64,18,4096]{2,1,0:T(8,128)(2,1)} %all_to_all.10) | data formatting | bytes 18874368 | tf_op jit(solution)/shard_map/reshape | solution.py:58
  551.6 0.0 copy-start.1
  551.6 0.0 copy-start.6
  551.6 8.7 %fusion.5 = f32[1152,384]{1,0:T(8,128)S(1)} fusion(bf16[1152,4096]{1,0:T(8,128)(2,1)} %reshape.115, bf16[1,4096,384]{2,1,0:T(8,128)(2,1)} %param.15), kind=kOutput, calls=%fused_computation.11 | convolution fusion | flops 3623878656 | bytes 14352384 | tf_op jit(solution)/shard_map/dot_general | solution.py:59
  560.3 0.0 copy-done.1
  560.3 0.0 copy-done.6
  560.3 6.2 fusion.7
  566.5 2.2 dot_general.17
  568.7 0.0 copy-done
  568.7 8.7 %convolution_convert_fusion = bf16[64,18,4096]{2,0,1:T(8,128)(2,1)} fusion(bf16[1,384,4096]{2,1,0:T(8,128)(2,1)S(1)} %copy-done, bf16[64,18,384]{2,1,0:T(8,128)(2,1)} %dot_general.17), kind=kOutput, calls=%fused_computation.3 | convolution fusion | flops 3628597248 | bytes 13467648 | tf_op jit(solution)/shard_map/dot_general | solution.py:62
  577.4 0.0 reduce-scatter.2.cloned.1.call-update
  577.4 87.9 %reduce-scatter.2.cloned.1.call-done = bf16[64,18,1024]{2,0,1:T(8,128)(2,1)} async-done(((bf16[64,18,4096]{2,0,1:T(8,128)(2,1)}), bf16[64,18,1024]{2,0,1:T(8,128)(2,1)}) %reduce-scatter.2.cloned.1.call-update) | async-done | bytes 2359312 | tf_op jit(solution)/shard_map/reduce_scatter | solution.py:64
  665.3 4.7 copy.27
  670.0 0.0 copy-start.5
  670.0 10.9 %all-to-all-start.1 = ((bf16[64,18,1024]{2,1,0:T(8,128)(2,1)}), bf16[64,18,1024]{2,1,0:T(8,128)(2,1)}, u32[]{:S(2)}, u32[]{:S(2)}) async-start(bf16[64,18,1024]{2,1,0:T(8,128)(2,1)} %copy.27), calls=%async_computation.2 | async-start | bytes 6291456 | tf_op jit(solution)/shard_map/all_to_all | solution.py:67
  680.9 0.0 copy-done.5
  680.9 0.1 copy.20
  681.0 73.5 %all-to-all-done.1 = bf16[64,18,1024]{2,1,0:T(8,128)(2,1)} async-done(((bf16[64,18,1024]{2,1,0:T(8,128)(2,1)}), bf16[64,18,1024]{2,1,0:T(8,128)(2,1)}, u32[]{:S(2)}, u32[]{:S(2)}) %all-to-all-start.1) | async-done | bytes 2359328 | tf_op jit(solution)/shard_map/all_to_all | solution.py:67
  754.6 4.3 reshape.116
  758.9 8.0 %gather_fusion.1 = bf16[1024,1024]{1,0:T(8,128)(2,1)} fusion(bf16[1152,1024]{1,0:T(8,128)(2,1)} %reshape.116, s32[1024]{0:T(1024)S(1)} %broadcast_clamp_fusion), kind=kCustom, calls=%fused_computation.1 | custom fusion | bytes 4198400 | tf_op jit(solution)/shard_map/gather | solution.py:68
  766.9 2.9 fusion.2
  769.8 1.7 add_convert_fusion.1
  (9 shorter events, 0.1 us)
Async XLA Ops:
  6.5 562.1 %copy-start = (bf16[1,384,4096]{2,1,0:T(8,128)(2,1)S(1)}, bf16[1,384,4096]{2,1,0:T(8,128)(2,1)}, u32[]{:S(2)}) copy-start(bf16[1,384,4096]{2,1,0:T(8,128)(2,1)} %param.17) | copy-start | bytes 9437188
  6.5 88.3 %all-gather.2.cloned.1.call-start = ((), (), s32[]{:S(2)}) async-start(), calls=%async_computation.3 | async-start | bytes 8519680 | tf_op jit(solution)/shard_map/all_gather | solution.py:28
  7.3 658.0 %reduce-scatter.2.cloned.1.call-start = ((), (), s32[]{:S(2)}) async-start(), calls=%async_computation.4 | async-start | bytes 11796480 | tf_op jit(solution)/shard_map/reduce_scatter | solution.py:64
  101.1 52.6 %copy-start.3 = (s32[128,8]{0,1:T(8,128)S(1)}, s32[128,8]{0,1:T(8,128)}, u32[]{:S(2)}) copy-start(s32[128,8]{0,1:T(8,128)} %param.13) | copy-start | bytes 12292
  101.2 52.8 %copy-start.4 = (bf16[4096]{0:T(1024)(128)(2,1)S(1)}, bf16[4096]{0:T(1024)(128)(2,1)}, u32[]{:S(2)}) copy-start(bf16[4096]{0:T(1024)(128)(2,1)} %param.12) | copy-start | bytes 24580
  101.2 47.9 %collective-permute-start = (f32[128,4096]{1,0:T(8,128)S(1)}, f32[128,4096]{1,0:T(8,128)S(1)}, u32[]{:S(2)}, u32[]{:S(2)}) collective-permute-start(f32[128,4096]{1,0:T(8,128)S(1)} %fusion.18), channel_id=1, source_target_pairs={{0,1},{1,0},{2,3},{3,2},{4,5},{5,4},{6,7},{7,6},{8,9},{9,8},{10,11... | collective-permute-start | bytes 6291464 | tf_op jit(solution)/shard_map/ppermute | solution.py:33
  150.7 48.8 %collective-permute-start.1 = (f32[128,4096]{1,0:T(8,128)}, f32[128,4096]{1,0:T(8,128)}, u32[]{:S(2)}, u32[]{:S(2)}) collective-permute-start(f32[128,4096]{1,0:T(8,128)} %add.74), channel_id=1, source_target_pairs={{0,2},{1,3},{2,0},{3,1},{4,6},{5,7},{6,4},{7,5},{8,10},{9,11},{10,... | collective-permute-start | bytes 6291464 | tf_op jit(solution)/shard_map/ppermute | solution.py:33
  202.5 1.1 copy-start.2
  551.6 8.7 %copy-start.1 = (bf16[1152,4096]{1,0:T(8,128)(2,1)S(1)}, bf16[1152,4096]{1,0:T(8,128)(2,1)}, u32[]{:S(2)}) copy-start(bf16[1152,4096]{1,0:T(8,128)(2,1)} %reshape.115) | copy-start | bytes 28311556
  551.6 8.7 %copy-start.6 = (bf16[1,4096,384]{2,1,0:T(8,128)(2,1)S(1)}, bf16[1,4096,384]{2,1,0:T(8,128)(2,1)}, u32[]{:S(2)}) copy-start(bf16[1,4096,384]{2,1,0:T(8,128)(2,1)} %param.16) | copy-start | bytes 9437188
  670.0 10.9 %copy-start.5 = (f32[128,8]{0,1:T(8,128)S(1)}, f32[128,8]{0,1:T(8,128)}, u32[]{:S(2)}) copy-start(f32[128,8]{0,1:T(8,128)} %param.14) | copy-start | bytes 12292
  670.0 84.5 %all-to-all-start.1 = ((bf16[64,18,1024]{2,1,0:T(8,128)(2,1)}), bf16[64,18,1024]{2,1,0:T(8,128)(2,1)}, u32[]{:S(2)}, u32[]{:S(2)}) async-start(bf16[64,18,1024]{2,1,0:T(8,128)(2,1)} %copy.27), calls=%async_computation.2 | async-start | bytes 6291456 | tf_op jit(solution)/shard_map/all_to_all | solution.py:67
Sparse Core Ops, SparseCore 0:
  10.1 84.6 all-gather.1
  577.5 87.7 reduce-scatter.1
